TPU v7x, 32 devices: a whole 2x2x4 slice. The times are simulated.
32 devices in a mesh: scene: 2 (over y), tok: 8 (over z, x), hid: 2 (over core).
Axes of the slice: x: 2, y: 2, z: 4, core: 2. Of those that a mesh axis runs over, the one named last changes fastest.
Arguments:
- input_keys: bfloat16 [16384, 384], P(('scene', 'tok'), 'hid'), parts along dimension 0, may hold values from -6 to 6
- input_values: bfloat16 [16384, 384], P(('scene', 'tok'), 'hid'), parts along dimension 0, may hold values from -6 to 6
- input_lr: float32 [16384], P(('scene', 'tok')), parts along dimension 0, may hold values from 0.1 to 1
- gate_weight: bfloat16 [384, 1536], P('tok', 'hid'), may hold values from -0.3125 to 0.3125
- up_weight: bfloat16 [384, 1536], P('tok', 'hid'), may hold values from -0.3125 to 0.3125
- down_weight: bfloat16 [384, 1536], P('tok', 'hid'), may hold values from -0.15625 to 0.15625
- queries: bfloat16 [2048, 384], P(('scene', 'tok'), 'hid'), parts along dimension 0, may hold values from -6 to 6
- out_grad: bfloat16 [2048, 384], P(('scene', 'tok'), 'hid'), parts along dimension 0, may hold values from -6 to 6
Outputs:
- target_out: bfloat16 [2048, 384], P(('scene', 'tok'), 'hid'), parts along dimension 0
- query_grad: bfloat16 [2048, 384], P(('scene', 'tok'), 'hid'), parts along dimension 0
There are 2 independent parts, one for each index of `scene`. A program takes and returns all parts, laid end to end along the dimension named above; an argument that names none is the same for every part. Nothing has to cross between parts.
All inputs are finite; a program needn't handle non-finite values.
Results may differ from a plain program's by a relative error of at most 0.009.
Values may be sent and summed in bfloat16 or wider, within the bound.
A program may use at most 64 MiB of HBM per device.

v0:
```python
import jax
import jax.numpy as jnp
from jax import lax
from jax.sharding import PartitionSpec as P

HID = 1536
step_ratio = 0.5
epsilon = 1e-06


def silu_slope(pre):
    sigma = jax.nn.sigmoid(pre)
    return sigma * (1.0 + pre * (1.0 - sigma))


def contract_rows(left, right):
    return lax.dot_general(
        left, right, (((0,), (0,)), ((), ())), preferred_element_type=jnp.float32
    )


def contract_cols(left, right):
    return lax.dot_general(
        left, right, (((1,), (1,)), ((), ())), preferred_element_type=jnp.float32
    )


def finish(moved, wsq, msq):
    return (moved * (jnp.sqrt(wsq) / jnp.sqrt(msq + epsilon))[:, None]).astype(jnp.bfloat16)


def shards(
    input_keys, input_values, input_lr, gate_weight, up_weight, down_weight, queries, out_grad
):
    keys, values = (
        lax.all_gather(input_keys, "hid", axis=1, tiled=True),
        lax.all_gather(input_values, "hid", axis=1, tiled=True),
    )
    w_gate, w_up, w_down = (
        lax.all_gather(gate_weight, "tok", axis=0, tiled=True),
        lax.all_gather(up_weight, "tok", axis=0, tiled=True),
        lax.all_gather(down_weight, "tok", axis=0, tiled=True),
    )
    scaled = (input_lr[:, None] * values.astype(jnp.float32)).astype(jnp.bfloat16)
    key_gate = jnp.dot(keys, w_gate, preferred_element_type=jnp.float32)
    key_up = jnp.dot(keys, w_up, preferred_element_type=jnp.float32)
    gate_act = jax.nn.silu(key_gate)
    key_act = (gate_act * key_up).astype(jnp.bfloat16)
    back = jnp.dot(scaled, w_down, preferred_element_type=jnp.float32)
    d_gate = (-back * key_up * silu_slope(key_gate)).astype(jnp.bfloat16)
    d_up = (-back * gate_act).astype(jnp.bfloat16)
    width = gate_weight.shape[1]
    grads = lax.psum(
        jnp.concatenate(
            [
                contract_rows(keys, d_gate),
                contract_rows(keys, d_up),
                -contract_rows(scaled, key_act),
            ],
            axis=1,
        ),
        "tok",
    )
    olds = (w_gate, w_up, w_down)
    pieces = [grads[:, :width], grads[:, width : 2 * width], grads[:, 2 * width :]]
    weights = [old.astype(jnp.float32) for old in olds]
    renewed = []
    stats = []
    for weight, grad in zip(weights, pieces):
        stats.append(jnp.sum(weight * weight, axis=1))
        stats.append(jnp.sum(weight * grad, axis=1))
        stats.append(jnp.sum(grad * grad, axis=1))
    totals = lax.psum(
        (stats[0], stats[1], stats[2], stats[3], stats[4], stats[5], stats[6], stats[7], stats[8]),
        "hid",
    )
    for index in range(3):
        wsq = totals[3 * index] / HID
        cross = totals[3 * index + 1] / HID
        gsq = totals[3 * index + 2] / HID
        scale = step_ratio * jnp.sqrt(wsq) / jnp.sqrt(gsq + epsilon)
        moved = weights[index] - scale[:, None] * pieces[index]
        msq = wsq - 2.0 * scale * cross + scale * scale * gsq
        renewed.append(finish(moved, wsq, msq))
    new_gate, new_up, new_down = (renewed[0], renewed[1], renewed[2])
    query_rows, grad_rows = (
        lax.all_gather(queries, "hid", axis=1, tiled=True),
        lax.all_gather(out_grad, "hid", axis=1, tiled=True),
    )
    query_gate = jnp.dot(query_rows, new_gate, preferred_element_type=jnp.float32)
    query_up = jnp.dot(query_rows, new_up, preferred_element_type=jnp.float32)
    query_silu = jax.nn.silu(query_gate)
    query_act = (query_silu * query_up).astype(jnp.bfloat16)
    out_part = contract_cols(query_act, new_down)
    query_back = jnp.dot(grad_rows, new_down, preferred_element_type=jnp.float32)
    q_gate_grad = (query_back * query_up * silu_slope(query_gate)).astype(jnp.bfloat16)
    q_up_grad = (query_back * query_silu).astype(jnp.bfloat16)
    grad_part = contract_cols(q_gate_grad, new_gate) + contract_cols(q_up_grad, new_up)
    out_sum, grad_sum = (
        lax.psum_scatter(
            out_part.astype(jnp.bfloat16), "hid", scatter_dimension=1, tiled=True
        ).astype(jnp.float32),
        lax.psum_scatter(
            grad_part.astype(jnp.bfloat16), "hid", scatter_dimension=1, tiled=True
        ).astype(jnp.float32),
    )
    return (out_sum.astype(jnp.bfloat16), grad_sum.astype(jnp.bfloat16))


def solution(mesh):
    return jax.shard_map(
        shards,
        mesh=mesh,
        in_specs=(
            P(("scene", "tok"), "hid"),
            P(("scene", "tok"), "hid"),
            P(("scene", "tok")),
            P("tok", "hid"),
            P("tok", "hid"),
            P("tok", "hid"),
            P(("scene", "tok"), "hid"),
            P(("scene", "tok"), "hid"),
        ),
        out_specs=(P(("scene", "tok"), "hid"), P(("scene", "tok"), "hid")),
        check_vma=False,
    )
```

profile of v0, /device:TPU:0, one launch (start us, length us, event | category | flops | bytes accessed | tf_op | source)
XLA Modules:
  0.0 297.7 jit_solution(15559393787212214560)
XLA Ops:
  7.2 2.7 all_gather.24
  9.9 33.4 %all_gather.21 = bf16[384,768]{1,0:T(8,128)(2,1)S(1)} all-gather(bf16[48,768]{1,0:T(8,128)(2,1)} %param.11), channel_id=1, replica_groups=mesh['scene'=2,'tok'=8,'hid'=2] {'tok'}, dimensions={0}, use_global_device_ids=true | all-gather | bytes 663552 | tf_op jit(solution)/shard_map/all_gather | solution.py:40
  43.4 31.3 %all_gather.25 = bf16[384,768]{1,0:T(8,128)(2,1)S(1)} all-gather(bf16[48,768]{1,0:T(8,128)(2,1)S(1)} %copy-done.6), channel_id=1, replica_groups=mesh['scene'=2,'tok'=8,'hid'=2] {'tok'}, dimensions={0}, use_global_device_ids=true | all-gather | bytes 663552 | tf_op jit(solution)/shard_map/all_gather | solution.py:41
  75.7 1.0 fusion.33
  76.7 2.4 all_gather.22
  79.1 31.4 %all_gather.23 = bf16[384,768]{1,0:T(8,128)(2,1)S(1)} all-gather(bf16[48,768]{1,0:T(8,128)(2,1)S(1)} %copy-done.7), channel_id=1, replica_groups=mesh['scene'=2,'tok'=8,'hid'=2] {'tok'}, dimensions={0}, use_global_device_ids=true | all-gather | bytes 663552 | tf_op jit(solution)/shard_map/all_gather | solution.py:42
  110.5 1.0 fusion.20
  111.6 1.2 fusion.6
  112.8 1.5 fusion.4
  114.3 1.3 fusion.5
  115.6 2.0 pad_maximum_fusion
  117.7 1.1 copy.14
  118.8 1.1 copy.16
  119.8 1.1 copy.17
  121.0 2.0 all_gather.27
  123.0 2.0 all_gather.26
  125.0 132.9 %all-reduce.3.cloned.1.call-done = f32[384,2304]{0,1:T(8,128)} async-done(((f32[384,2304]{0,1:T(8,128)}), f32[384,2304]{0,1:T(8,128)}) %all-reduce.3.cloned.1.call-update) | async-done | bytes 3538960 | tf_op jit(solution)/shard_map/psum | solution.py:53
  257.9 4.1 %multiply_reduce_fusion.2 = (f32[384]{0:T(512)S(1)}, f32[384]{0:T(512)S(1)}, f32[384]{0:T(512)S(1)}, f32[384]{0:T(512)S(1)}, f32[384]{0:T(512)}, /*index=5*/f32[...) fusion(f32[384,2304]{0,1:T(8,128)} %all-reduce.3.cloned.1.call-done, bf16[384,768]{0,1:T(8,128)(2,1)} %copy.14, ...), kind=kLoop, calls=%fused_computation.39 | loop fusion | flops 6189696 | bytes 5322240 | tf_op jit(solution)/shard_map/reduce_sum | solution.py:72
  261.9 4.6 %all-reduce = (f32[384]{0:T(512)}, f32[384]{0:T(512)}, f32[384]{0:T(512)}, f32[384]{0:T(512)}, f32[384]{0:T(512)}, /*index=5*/f32[384]{0:T(512)}, f32[384]{0:T(512)}, f32[384]{0:T(512)}, f32[384]{0:T(512)}) all-reduce(f32[384]{0:T(512)S(1)} %get-tuple-element.5, ...), channel_id=1, replica_groups=mesh['scene'=2,'tok'=8,'hid'=2] {'hid'}, use_global_device_ids=true, to_apply=%region_18.19 | all-reduce | flops 3456 | bytes 27648 | tf_op jit(solution)/shard_map/psum | solution.py:73
  268.0 2.0 fusion.9
  271.8 1.1 fusion.19
  273.0 1.0 convolution_convert_fusion
  274.0 5.6 %reduce-scatter.5.cloned.1.call-done = bf16[128,192]{0,1:T(8,128)(2,1)} async-done(((bf16[128,384]{0,1:T(8,128)(2,1)}), bf16[128,192]{0,1:T(8,128)(2,1)}) %reduce-scatter.5.cloned.1.call-update) | async-done | bytes 49168 | tf_op jit(solution)/shard_map/reduce_scatter | solution.py:103
  279.7 11.5 %reduce-scatter.3.cloned.1.call-done = bf16[128,192]{0,1:T(8,128)(2,1)} async-done(((bf16[128,384]{0,1:T(8,128)(2,1)}), bf16[128,192]{0,1:T(8,128)(2,1)}) %reduce-scatter.3.cloned.1.call-update) | async-done | bytes 49168 | tf_op jit(solution)/shard_map/reduce_scatter | solution.py:100
  (35 shorter events, 4.4 us)
Async XLA Ops:
  7.2 36.2 %copy-start.6 = (bf16[48,768]{1,0:T(8,128)(2,1)S(1)}, bf16[48,768]{1,0:T(8,128)(2,1)}, u32[]{:S(2)}) copy-start(bf16[48,768]{1,0:T(8,128)(2,1)} %param.12) | copy-start | bytes 221188
  7.2 250.7 %all-reduce.3.cloned.1.call-start = ((), (), s32[]{:S(2)}) async-start(), calls=%async_computation.2 | async-start | bytes 7077888 | tf_op jit(solution)/shard_map/psum | solution.py:53
  75.7 1.1 copy-start.5
  75.7 3.4 %copy-start.7 = (bf16[48,768]{1,0:T(8,128)(2,1)S(1)}, bf16[48,768]{1,0:T(8,128)(2,1)}, u32[]{:S(2)}) copy-start(bf16[48,768]{1,0:T(8,128)(2,1)} %param.13) | copy-start | bytes 221188
  76.7 33.8 %copy-start.10 = (f32[1024]{0:T(1024)S(1)}, f32[1024]{0:T(1024)}, u32[]{:S(2)}) copy-start(f32[1024]{0:T(1024)} %param.10) | copy-start | bytes 12292
  117.7 3.3 %copy-start.8 = (bf16[128,192]{0,1:T(8,128)(2,1)S(1)}, bf16[128,192]{0,1:T(8,128)(2,1)}, u32[]{:S(2)}) copy-start(bf16[128,192]{0,1:T(8,128)(2,1)} %param.15) | copy-start | bytes 147460
  117.7 5.3 %copy-start.9 = (bf16[128,192]{0,1:T(8,128)(2,1)S(1)}, bf16[128,192]{0,1:T(8,128)(2,1)}, u32[]{:S(2)}) copy-start(bf16[128,192]{0,1:T(8,128)(2,1)} %param.14) | copy-start | bytes 147460
  117.7 162.0 %reduce-scatter.5.cloned.1.call-start = ((), (), s32[]{:S(2)}) async-start(), calls=%async_computation.4 | async-start | bytes 147456 | tf_op jit(solution)/shard_map/reduce_scatter | solution.py:103
  257.8 10.2 %copy-start = (f32[384,2304]{0,1:T(8,128)S(1)}, f32[384,2304]{0,1:T(8,128)}, u32[]{:S(2)}) copy-start(f32[384,2304]{0,1:T(8,128)} %all-reduce.3.cloned.1.call-done) | copy-start | bytes 10616836
  268.0 2.1 copy-start.3
  270.0 1.3 copy-start.1
  270.1 1.0 copy-start.4
  271.8 1.2 copy-start.2
  272.9 18.2 %reduce-scatter.3.cloned.1.call-start = ((), (), s32[]{:S(2)}) async-start(), calls=%async_computation.3 | async-start | bytes 147456 | tf_op jit(solution)/shard_map/reduce_scatter | solution.py:100
Sparse Core Ops, SparseCore 0:
  117.8 140.0 all-reduce.2
  273.1 6.5 reduce-scatter.4
  282.5 8.6 reduce-scatter.2
where the time goes:
time: 298 us
  waiting for transfers between devices  150 us (50%)
  blocking collectives  110 us (37%)
  between operations  13.9 us (5%)
  matrix products  10.6 us (4%)
  other arithmetic  9.59 us (3%)
  local copies, waits for them, and re-layouts  3.61 us (1%)
    psum x1, waiting for transfers between devices, shards(): lax.psum(jnp.concatenate([contract_rows(keys, d_gate), contract_rows(keys...  133 us
    all_gather x1, blocking collectives, shards(): lax.all_gather(gate_weight, 'tok', axis=0, tiled=True)  33.4 us
    all_gather x1, blocking collectives, shards(): lax.all_gather(down_weight, 'tok', axis=0, tiled=True)  31.4 us
    all_gather x1, blocking collectives, shards(): lax.all_gather(up_weight, 'tok', axis=0, tiled=True)  31.3 us
    reduce_scatter x1, waiting for transfers between devices, shards(): lax.psum_scatter(out_part.astype(jnp.bfloat16), 'hid', scatter_dimension=...  11.5 us
  transfers between devices with their start and end apart: 3, of which 3 were waited for; matrix products, arithmetic and copies ran while one was open for 1% of the time, Pallas kernels for 0%

commit v1 on v0

--- a/solution.py
+++ b/solution.py
@@ -6,6 +6,22 @@
 HID = 1536
 step_ratio = 0.5
 epsilon = 1e-06
+
+
+def gather_around(x, axis, dim):
+    ways, here, step = (lax.axis_size(axis), lax.axis_index(axis), x.shape[dim])
+    dims = [n * ways if d == dim else n for d, n in enumerate(x.shape)]
+    full = lax.dynamic_update_slice_in_dim(jnp.zeros(dims, x.dtype), x, here * step, axis=dim)
+    going_up = going_down = x
+    for far in range(1, ways // 2 + 1):
+        going_up = lax.ppermute(going_up, axis, [(d, (d + 1) % ways) for d in range(ways)])
+        full = lax.dynamic_update_slice_in_dim(full, going_up, (here - far) % ways * step, axis=dim)
+        if 2 * far < ways:
+            going_down = lax.ppermute(going_down, axis, [(d, (d - 1) % ways) for d in range(ways)])
+            full = lax.dynamic_update_slice_in_dim(
+                full, going_down, (here + far) % ways * step, axis=dim
+            )
+    return full
 
 
 def silu_slope(pre):
@@ -38,7 +54,7 @@
     )
     w_gate, w_up, w_down = (
         lax.all_gather(gate_weight, "tok", axis=0, tiled=True),
-        lax.all_gather(up_weight, "tok", axis=0, tiled=True),
+        gather_around(up_weight, "tok", 0),
         lax.all_gather(down_weight, "tok", axis=0, tiled=True),
     )
     scaled = (input_lr[:, None] * values.astype(jnp.float32)).astype(jnp.bfloat16)

time: 298 us -> 318 us (1.067)
  blocking collectives: 110 us -> 77.1 us
  local copies, waits for them, and re-layouts: 3.61 us -> 31 us
  starting transfers between devices: 0.12 us -> 16.3 us
  waiting for transfers between devices: 150 us -> 155 us
    all_gather x1 -> x0, blocking collectives: 31.3 us -> none  [shards(): lax.all_gather(up_weight, 'tok', axis=0, tiled=True)]
    dynamic_update_slice x0 -> x8, local copies, waits for them, and re-layouts: none -> 26.3 us  [the longest x4 13.6 us: gather_around(): lax.dynamic_update_slice_in_dim(full, going_up, (here - far) % ways * ste...]
    ppermute x0 -> x7, starting transfers between devices: none -> 16.2 us  [the longest x3 13.2 us: gather_around(): lax.ppermute(going_down, axis, [(d, (d - 1) % ways) for d in range(ways)])]
    ppermute x0 -> x7, waiting for transfers between devices: none -> 3.42 us  [the longest x3 2.02 us: gather_around(): lax.ppermute(going_down, axis, [(d, (d - 1) % ways) for d in range(ways)])]
  transfers between devices with their start and end apart: 3 -> 10, of which waited for: 3 -> 5; matrix products, arithmetic and copies ran while one was open for 1% -> 10% of each run, Pallas kernels for 0% -> 0%
where the time goes in v1:
time: 318 us; the launch traced here: 317 us
  waiting for transfers between devices  155 us (49%)
  blocking collectives  77.1 us (24%)
  local copies, waits for them, and re-layouts  31 us (10%)
  starting transfers between devices  16.3 us (5%)
  between operations  14.2 us (4%)
  matrix products  13.7 us (4%)
  other arithmetic  9.62 us (3%)
    psum x1, waiting for transfers between devices, shards(): lax.psum(jnp.concatenate([contract_rows(keys, d_gate), contract_rows(keys...  134 us
    all_gather x1, blocking collectives, shards(): lax.all_gather(down_weight, 'tok', axis=0, tiled=True)  31.8 us
    all_gather x1, blocking collectives, shards(): lax.all_gather(gate_weight, 'tok', axis=0, tiled=True)  31.5 us
    dynamic_update_slice x4, local copies, waits for them, and re-layouts, gather_around(): lax.dynamic_update_slice_in_dim(full, going_up, (here - far) % ways * ste...  13.6 us
    ppermute x3, starting transfers between devices, gather_around(): lax.ppermute(going_down, axis, [(d, (d - 1) % ways) for d in range(ways)])  13.2 us
    reduce_scatter x1, waiting for transfers between devices, shards(): lax.psum_scatter(out_part.astype(jnp.bfloat16), 'hid', scatter_dimension=...  11.5 us
    dynamic_update_slice x3, local copies, waits for them, and re-layouts, gather_around(): lax.dynamic_update_slice_in_dim(full, going_down, (here + far) % ways * s...  10.6 us
    dot_general x3, matrix products, contract_rows(): lax.dot_general(left, right, (((0,), (0,)), ((), ())), preferred_element_...  7.17 us
  transfers between devices with their start and end apart: 10, of which 5 were waited for; matrix products, arithmetic and copies ran while one was open for 10% of the time, Pallas kernels for 0%

profile of v1, /device:TPU:0, one launch (start us, length us, event | category | flops | bytes accessed | tf_op | source)
XLA Modules:
  0.0 316.7 jit_solution(12454617680478117471)
XLA Ops:
  8.3 3.0 collective-permute-start
  11.3 3.1 collective-permute-start.1
  14.4 2.6 all_gather.19
  17.0 31.8 %all_gather.20 = bf16[384,768]{1,0:T(8,128)(2,1)S(1)} all-gather(bf16[48,768]{1,0:T(8,128)(2,1)} %param.13), channel_id=1, replica_groups=mesh['scene'=2,'tok'=8,'hid'=2] {'tok'}, dimensions={0}, use_global_device_ids=true | all-gather | bytes 663552 | tf_op jit(solution)/shard_map/all_gather | solution.py:58
  49.8 31.5 %all_gather.18 = bf16[384,768]{1,0:T(8,128)(2,1)S(1)} all-gather(bf16[48,768]{1,0:T(8,128)(2,1)S(1)} %copy-done.15), channel_id=1, replica_groups=mesh['scene'=2,'tok'=8,'hid'=2] {'tok'}, dimensions={0}, use_global_device_ids=true | all-gather | bytes 663552 | tf_op jit(solution)/shard_map/all_gather | solution.py:56
  81.4 2.4 all_gather.21
  83.8 4.7 %collective-permute-start.3 = (bf16[48,768]{0,1:T(8,128)(2,1)S(1)}, bf16[48,768]{0,1:T(8,128)(2,1)}, u32[]{:S(2)}, u32[]{:S(2)}) collective-permute-start(bf16[48,768]{0,1:T(8,128)(2,1)S(1)} %collective-permute-done.1), channel_id=1, source_target_pairs={{0,14},{2,0},{4,2},{6,4},{8,6},{10,8},{12,10},{14,12},{1,15},{3,1}... | collective-permute-start | bytes 221192 | tf_op jit(solution)/shard_map/ppermute | solution.py:20
  92.9 5.4 %collective-permute-start.5 = (bf16[48,768]{0,1:T(8,128)(2,1)}, bf16[48,768]{0,1:T(8,128)(2,1)}, u32[]{:S(2)}, u32[]{:S(2)}) collective-permute-start(bf16[48,768]{0,1:T(8,128)(2,1)} %collective-permute-done.3), channel_id=1, source_target_pairs={{0,14},{2,0},{4,2},{6,4},{8,6},{10,8},{12,10},{14,12},{1,15},{3,1}... | collective-permute-start | bytes 221192 | tf_op jit(solution)/shard_map/ppermute | solution.py:20
  98.3 2.2 fusion.15
  102.7 3.3 %dynamic_update_slice.25 = bf16[384,768]{0,1:T(8,128)(2,1)S(1)} dynamic-update-slice(bf16[384,768]{0,1:T(8,128)(2,1)S(1)} %dynamic_update_slice.24, bf16[48,768]{0,1:T(8,128)(2,1)} %copy-done.12, s32[]{:T(128)S(6)} %select_n.57, s32[]{:T(128)} %constant.77.clone.1) | dynamic-update-slice | bytes 147460 | tf_op jit(solution)/shard_map/dynamic_update_slice | solution.py:18
  106.0 3.5 %dynamic_update_slice.26 = bf16[384,768]{0,1:T(8,128)(2,1)S(1)} dynamic-update-slice(bf16[384,768]{0,1:T(8,128)(2,1)S(1)} %dynamic_update_slice.25, bf16[48,768]{0,1:T(8,128)(2,1)} %copy-done.13, s32[]{:T(128)S(6)} %select_n.59, s32[]{:T(128)} %constant.77.clone.1) | dynamic-update-slice | bytes 147460 | tf_op jit(solution)/shard_map/dynamic_update_slice | solution.py:21
  109.5 3.3 %dynamic_update_slice.27 = bf16[384,768]{0,1:T(8,128)(2,1)S(1)} dynamic-update-slice(bf16[384,768]{0,1:T(8,128)(2,1)S(1)} %dynamic_update_slice.26, bf16[48,768]{0,1:T(8,128)(2,1)} %copy-done.14, s32[]{:T(128)S(6)} %select_n.61, s32[]{:T(128)} %constant.77.clone.1) | dynamic-update-slice | bytes 147460 | tf_op jit(solution)/shard_map/dynamic_update_slice | solution.py:18
  112.8 3.5 %dynamic_update_slice.28 = bf16[384,768]{0,1:T(8,128)(2,1)S(1)} dynamic-update-slice(bf16[384,768]{0,1:T(8,128)(2,1)S(1)} %dynamic_update_slice.27, bf16[48,768]{0,1:T(8,128)(2,1)} %collective-permute-done.3, s32[]{:T(128)S(6)} %select_n.63, s32[]{:T(128)} %constant.77.clone.1) | dynamic-update-slice | bytes 147460 | tf_op jit(solution)/shard_map/dynamic_update_slice | solution.py:21
  116.4 3.5 %dynamic_update_slice.29 = bf16[384,768]{0,1:T(8,128)(2,1)S(1)} dynamic-update-slice(bf16[384,768]{0,1:T(8,128)(2,1)S(1)} %dynamic_update_slice.28, bf16[48,768]{0,1:T(8,128)(2,1)} %collective-permute-done.4, s32[]{:T(128)S(6)} %select_n.65, s32[]{:T(128)} %constant.77.clone.1) | dynamic-update-slice | bytes 147460 | tf_op jit(solution)/shard_map/dynamic_update_slice | solution.py:18
  119.9 3.5 %dynamic_update_slice.30 = bf16[384,768]{0,1:T(8,128)(2,1)S(1)} dynamic-update-slice(bf16[384,768]{0,1:T(8,128)(2,1)S(1)} %dynamic_update_slice.29, bf16[48,768]{0,1:T(8,128)(2,1)} %collective-permute-done.5, s32[]{:T(128)S(6)} %select_n.67, s32[]{:T(128)} %constant.77.clone.1) | dynamic-update-slice | bytes 147460 | tf_op jit(solution)/shard_map/dynamic_update_slice | solution.py:21
  123.5 3.5 %dynamic_update_slice.31 = bf16[384,768]{0,1:T(8,128)(2,1)S(1)} dynamic-update-slice(bf16[384,768]{0,1:T(8,128)(2,1)S(1)} %dynamic_update_slice.30, bf16[48,768]{0,1:T(8,128)(2,1)} %collective-permute-done.6, s32[]{:T(128)S(6)} %select_n.69, s32[]{:T(128)} %constant.77.clone.1) | dynamic-update-slice | bytes 147460 | tf_op jit(solution)/shard_map/dynamic_update_slice | solution.py:18
  129.1 3.6 %fusion.9 = f32[384,768]{0,1:T(8,128)S(1)} fusion(bf16[1024,384]{0,1:T(8,128)(2,1)S(1)} %all_gather.21, f32[768,1024]{0,1:T(8,128)S(1)} %fusion.42, f32[1024,768]{1,0:T(8,128)} %copy-done.4, f32[1024,768]{1,0:T(8,128)S(1)} %copy-done.3), kind=kOutput, calls=%fused_computation.22 | convolution fusion | flops 612630528 | bytes 11403264 | tf_op jit(solution)/shard_map/dot_general | solution.py:33
  134.1 2.1 pad_maximum_fusion
  140.4 2.2 all_gather.22
  142.6 134.2 %all-reduce.3.cloned.1.call-done = f32[384,2304]{0,1:T(8,128)} async-done(((f32[384,2304]{0,1:T(8,128)}), f32[384,2304]{0,1:T(8,128)}) %all-reduce.3.cloned.1.call-update) | async-done | bytes 3538960 | tf_op jit(solution)/shard_map/psum | solution.py:69
  276.9 4.1 %multiply_reduce_fusion.2 = (f32[384]{0:T(512)S(1)}, f32[384]{0:T(512)S(1)}, f32[384]{0:T(512)S(1)}, f32[384]{0:T(512)S(1)}, f32[384]{0:T(512)}, /*index=5*/f32[...) fusion(f32[384,2304]{0,1:T(8,128)} %all-reduce.3.cloned.1.call-done, bf16[384,768]{0,1:T(8,128)(2,1)} %copy.17, ...), kind=kLoop, calls=%fused_computation.42 | loop fusion | flops 6189696 | bytes 5322240 | tf_op jit(solution)/shard_map/reduce_sum | solution.py:88
  280.9 4.6 %all-reduce = (f32[384]{0:T(512)}, f32[384]{0:T(512)}, f32[384]{0:T(512)}, f32[384]{0:T(512)}, f32[384]{0:T(512)}, /*index=5*/f32[384]{0:T(512)}, f32[384]{0:T(512)}, f32[384]{0:T(512)}, f32[384]{0:T(512)}) all-reduce(f32[384]{0:T(512)S(1)} %get-tuple-element.5, ...), channel_id=1, replica_groups=mesh['scene'=2,'tok'=8,'hid'=2] {'hid'}, use_global_device_ids=true, to_apply=%region_18.19 | all-reduce | flops 3456 | bytes 27648 | tf_op jit(solution)/shard_map/psum | solution.py:89
  293.1 5.6 %reduce-scatter.5.cloned.1.call-done = bf16[128,192]{0,1:T(8,128)(2,1)} async-done(((bf16[128,384]{0,1:T(8,128)(2,1)}), bf16[128,192]{0,1:T(8,128)(2,1)}) %reduce-scatter.5.cloned.1.call-update) | async-done | bytes 49168 | tf_op jit(solution)/shard_map/reduce_scatter | solution.py:119
  298.7 11.5 %reduce-scatter.3.cloned.1.call-done = bf16[128,192]{0,1:T(8,128)(2,1)} async-done(((bf16[128,384]{0,1:T(8,128)(2,1)}), bf16[128,192]{0,1:T(8,128)(2,1)}) %reduce-scatter.3.cloned.1.call-update) | async-done | bytes 49168 | tf_op jit(solution)/shard_map/reduce_scatter | solution.py:116
  (73 shorter events, 23.7 us)
Async XLA Ops:
  7.2 41.6 %copy-start.18 = (f32[1024]{0:T(1024)S(1)}, f32[1024]{0:T(1024)}, u32[]{:S(2)}) copy-start(f32[1024]{0:T(1024)} %param.10) | copy-start | bytes 12292
  7.2 269.7 %all-reduce.3.cloned.1.call-start = ((), (), s32[]{:S(2)}) async-start(), calls=%async_computation.2 | async-start | bytes 7077888 | tf_op jit(solution)/shard_map/psum | solution.py:69
  8.3 73.1 %collective-permute-start = (bf16[48,768]{0,1:T(8,128)(2,1)S(1)}, bf16[48,768]{0,1:T(8,128)(2,1)S(1)}, u32[]{:S(2)}, u32[]{:S(2)}) collective-permute-start(bf16[48,768]{0,1:T(8,128)(2,1)S(1)} %copy.18), channel_id=1, source_target_pairs={{0,2},{2,4},{4,6},{6,8},{8,10},{10,12},{12,14},{14,0},{1,3},{3,5},... | collective-permute-start | bytes 221192 | tf_op jit(solution)/shard_map/ppermute | solution.py:17
  11.3 72.5 %collective-permute-start.1 = (bf16[48,768]{0,1:T(8,128)(2,1)S(1)}, bf16[48,768]{0,1:T(8,128)(2,1)S(1)}, u32[]{:S(2)}, u32[]{:S(2)}) collective-permute-start(bf16[48,768]{0,1:T(8,128)(2,1)S(1)} %copy.18), channel_id=1, source_target_pairs={{0,14},{2,0},{4,2},{6,4},{8,6},{10,8},{12,10},{14,12},{1,15},{3,1}... | collective-permute-start | bytes 221192 | tf_op jit(solution)/shard_map/ppermute | solution.py:20
  48.8 32.6 %copy-start.11 = (bf16[1024,192]{0,1:T(8,128)(2,1)S(1)}, bf16[1024,192]{0,1:T(8,128)(2,1)}, u32[]{:S(2)}) copy-start(bf16[1024,192]{0,1:T(8,128)(2,1)} %param.8) | copy-start | bytes 1179652
  49.8 48.5 %copy-start.2 = (f32[1024,768]{1,0:T(8,128)}, f32[1024,768]{1,0:T(8,128)S(1)}, u32[]{:S(2)}) copy-start(f32[1024,768]{1,0:T(8,128)S(1)} %fusion.29) | copy-start | bytes 9437188
  81.4 9.5 %copy-start.12 = (bf16[48,768]{0,1:T(8,128)(2,1)}, bf16[48,768]{0,1:T(8,128)(2,1)S(1)}, u32[]{:S(2)}) copy-start(bf16[48,768]{0,1:T(8,128)(2,1)S(1)} %collective-permute-done) | copy-start | bytes 221188
  81.4 8.5 %collective-permute-start.2 = (bf16[48,768]{0,1:T(8,128)(2,1)S(1)}, bf16[48,768]{0,1:T(8,128)(2,1)S(1)}, u32[]{:S(2)}, u32[]{:S(2)}) collective-permute-start(bf16[48,768]{0,1:T(8,128)(2,1)S(1)} %collective-permute-done), channel_id=1, source_target_pairs={{0,2},{2,4},{4,6},{6,8},{8,10},{10,12},{12,14},{14,0},{1,3},{3,5},... | collective-permute-start | bytes 221192 | tf_op jit(solution)/shard_map/ppermute | solution.py:17
  83.8 7.1 %copy-start.13 = (bf16[48,768]{0,1:T(8,128)(2,1)}, bf16[48,768]{0,1:T(8,128)(2,1)S(1)}, u32[]{:S(2)}) copy-start(bf16[48,768]{0,1:T(8,128)(2,1)S(1)} %collective-permute-done.1) | copy-start | bytes 221188
  83.8 9.2 %collective-permute-start.3 = (bf16[48,768]{0,1:T(8,128)(2,1)S(1)}, bf16[48,768]{0,1:T(8,128)(2,1)}, u32[]{:S(2)}, u32[]{:S(2)}) collective-permute-start(bf16[48,768]{0,1:T(8,128)(2,1)S(1)} %collective-permute-done.1), channel_id=1, source_target_pairs={{0,14},{2,0},{4,2},{6,4},{8,6},{10,8},{12,10},{14,12},{1,15},{3,1}... | collective-permute-start | bytes 221192 | tf_op jit(solution)/shard_map/ppermute | solution.py:20
  89.8 8.5 %collective-permute-start.4 = (bf16[48,768]{0,1:T(8,128)(2,1)S(1)}, bf16[48,768]{0,1:T(8,128)(2,1)}, u32[]{:S(2)}, u32[]{:S(2)}) collective-permute-start(bf16[48,768]{0,1:T(8,128)(2,1)S(1)} %collective-permute-done.2), channel_id=1, source_target_pairs={{0,2},{2,4},{4,6},{6,8},{8,10},{10,12},{12,14},{14,0},{1,3},{3,5},... | collective-permute-start | bytes 221192 | tf_op jit(solution)/shard_map/ppermute | solution.py:17
  90.9 9.7 %copy-start.4 = (f32[1024,768]{1,0:T(8,128)}, f32[1024,768]{1,0:T(8,128)S(1)}, u32[]{:S(2)}) copy-start(f32[1024,768]{1,0:T(8,128)S(1)} %fusion.43) | copy-start | bytes 9437188
  92.9 27.0 %collective-permute-start.5 = (bf16[48,768]{0,1:T(8,128)(2,1)}, bf16[48,768]{0,1:T(8,128)(2,1)}, u32[]{:S(2)}, u32[]{:S(2)}) collective-permute-start(bf16[48,768]{0,1:T(8,128)(2,1)} %collective-permute-done.3), channel_id=1, source_target_pairs={{0,14},{2,0},{4,2},{6,4},{8,6},{10,8},{12,10},{14,12},{1,15},{3,1}... | collective-permute-start | bytes 221192 | tf_op jit(solution)/shard_map/ppermute | solution.py:20
  98.3 25.1 %collective-permute-start.6 = (bf16[48,768]{0,1:T(8,128)(2,1)}, bf16[48,768]{0,1:T(8,128)(2,1)}, u32[]{:S(2)}, u32[]{:S(2)}) collective-permute-start(bf16[48,768]{0,1:T(8,128)(2,1)} %collective-permute-done.4), channel_id=1, source_target_pairs={{0,2},{2,4},{4,6},{6,8},{8,10},{10,12},{12,14},{14,0},{1,3},{3,5},... | collective-permute-start | bytes 221192 | tf_op jit(solution)/shard_map/ppermute | solution.py:17
  127.0 2.1 copy-start.3
  129.1 3.6 %copy-start.5 = (f32[1024,768]{1,0:T(8,128)S(1)}, f32[1024,768]{1,0:T(8,128)}, u32[]{:S(2)}) copy-start(f32[1024,768]{1,0:T(8,128)} %copy-done.4) | copy-start | bytes 9437188
  132.7 1.4 copy-start.8
  136.2 2.2 copy-start.16
  136.2 4.2 %copy-start.17 = (bf16[128,192]{0,1:T(8,128)(2,1)S(1)}, bf16[128,192]{0,1:T(8,128)(2,1)}, u32[]{:S(2)}) copy-start(bf16[128,192]{0,1:T(8,128)(2,1)} %param.14) | copy-start | bytes 147460
  136.2 162.5 %reduce-scatter.5.cloned.1.call-start = ((), (), s32[]{:S(2)}) async-start(), calls=%async_computation.4 | async-start | bytes 147456 | tf_op jit(solution)/shard_map/reduce_scatter | solution.py:119
  276.9 10.1 %copy-start = (f32[384,2304]{0,1:T(8,128)S(1)}, f32[384,2304]{0,1:T(8,128)}, u32[]{:S(2)}) copy-start(f32[384,2304]{0,1:T(8,128)} %all-reduce.3.cloned.1.call-done) | copy-start | bytes 10616836
  287.0 2.1 copy-start.9
  289.1 1.3 copy-start.6
  291.9 18.2 %reduce-scatter.3.cloned.1.call-start = ((), (), s32[]{:S(2)}) async-start(), calls=%async_computation.3 | async-start | bytes 147456 | tf_op jit(solution)/shard_map/reduce_scatter | solution.py:116
  (5 other events, 5.3 us)
Sparse Core Ops, SparseCore 0:
  136.3 140.4 all-reduce.2
  292.1 6.5 reduce-scatter.4
  301.5 8.6 reduce-scatter.2
